TPU v7x, 32 devices: a whole 2x2x4 slice. The times are simulated.
32 devices in a mesh: fsdp: 4 (over y, x), ctx: 2 (over core), tp: 4 (over z).
Axes of the slice: x: 2, y: 2, z: 4, core: 2. Of those that a mesh axis runs over, the one named last changes fastest.
Arguments:
- tokens: bfloat16 [4, 2048, 2048], P('fsdp', 'ctx'), may hold values from -6 to 6
- cotangent: bfloat16 [4, 2048, 2048], P('fsdp', 'ctx'), may hold values from -6 to 6
- piece_starts: int32 [4, 3], P('fsdp'), may hold values from 0 to 1790, as said below
- attn_gain: bfloat16 [2048], P(('fsdp', 'ctx')), may hold values from 0.5 to 1.5
- query_down: bfloat16 [2048, 1024], P(('fsdp', 'ctx')), may hold values from -0.125 to 0.125
- query_gain: bfloat16 [1024], P(('fsdp', 'ctx')), may hold values from 0.5 to 1.5
- query_up: bfloat16 [1024, 4096], P(('fsdp', 'ctx'), 'tp'), may hold values from -0.1875 to 0.1875
- key_proj: bfloat16 [2048, 256], P(('fsdp', 'ctx')), may hold values from -0.125 to 0.125
- value_proj: bfloat16 [2048, 256], P(('fsdp', 'ctx')), may hold values from -0.125 to 0.125
- out_proj: bfloat16 [4096, 2048], P('tp', ('fsdp', 'ctx')), may hold values from -1 to 1
- ffn_gain: bfloat16 [2048], P(('fsdp', 'ctx')), may hold values from 0.5 to 1.5
- gate_proj: bfloat16 [2048, 5632], P(('fsdp', 'ctx'), 'tp'), may hold values from -0.125 to 0.125
- up_proj: bfloat16 [2048, 5632], P(('fsdp', 'ctx'), 'tp'), may hold values from -0.125 to 0.125
- down_proj: bfloat16 [5632, 2048], P('tp', ('fsdp', 'ctx')), may hold values from -0.078125 to 0.078125
Outputs:
- layer_out: bfloat16 [4, 2048, 2048], P('fsdp', 'ctx')
- tokens_grad: bfloat16 [4, 2048, 2048], P('fsdp', 'ctx')
- attn_gain_grad: float32 [2048], P(('fsdp', 'ctx'))
- query_down_grad: float32 [2048, 1024], P(('fsdp', 'ctx'))
- query_gain_grad: float32 [1024], P(('fsdp', 'ctx'))
- query_up_grad: float32 [1024, 4096], P(('fsdp', 'ctx'), 'tp')
- key_proj_grad: float32 [2048, 256], P(('fsdp', 'ctx'))
- value_proj_grad: float32 [2048, 256], P(('fsdp', 'ctx'))
- out_proj_grad: float32 [4096, 2048], P('tp', ('fsdp', 'ctx'))
- ffn_gain_grad: float32 [2048], P(('fsdp', 'ctx'))
- gate_proj_grad: float32 [2048, 5632], P(('fsdp', 'ctx'), 'tp')
- up_proj_grad: float32 [2048, 5632], P(('fsdp', 'ctx'), 'tp')
- down_proj_grad: float32 [5632, 2048], P('tp', ('fsdp', 'ctx'))
Inputs may be any that keep to these rules, and one draw needn't show every extreme that they name: `piece_starts`: in each sequence piece k starts at or after k * (682) and ends by (k + 1) * 682, so pieces never intersect and starts rise.
All inputs are finite; a program needn't handle non-finite values.
Results may differ from a plain program's by a relative error of at most 0.024.
Values may be sent and summed in bfloat16 or wider, within the bound.
No kernel may reach another device: no remote copies, remote signals or barrier semaphores. Data moves between devices by JAX's collectives and lax.ppermute only.
A program may use at most 256 MiB of HBM per device.

v0:
```python
import jax
import jax.numpy as jnp
from jax import lax
from jax.sharding import PartitionSpec as P

PIECE = 256
norm_eps = 1e-05
masked_score = -1e30


def rope_tables(positions, width):
    half_width = width // 2
    freqs = jnp.exp(-jnp.log(10000.0) * jnp.arange(half_width).astype(jnp.float32) * 2.0 / width)
    angles = positions.astype(jnp.float32)[:, None] * freqs[None, :]
    return (jnp.cos(angles), jnp.sin(angles))


def rotate(vectors, cosine, sine):
    half_width = vectors.shape[-1] // 2
    first, second = (vectors[..., :half_width], vectors[..., half_width:])
    return jnp.concatenate(
        [first * cosine - second * sine, second * cosine + first * sine], axis=-1
    )


def unrotate(vectors, cosine, sine):
    half_width = vectors.shape[-1] // 2
    first, second = (vectors[..., :half_width], vectors[..., half_width:])
    return jnp.concatenate(
        [first * cosine + second * sine, second * cosine - first * sine], axis=-1
    )


def piece_ids(positions, starts):
    inside = (positions[:, None] >= starts[None, :]) & (
        positions[:, None] < starts[None, :] + PIECE
    )
    numbers = jnp.arange(1, starts.shape[0] + 1)
    return jnp.sum(jnp.where(inside, numbers[None, :], 0), axis=1) - 1


def normalize(values, norm_weight):
    inverse = lax.rsqrt(jnp.mean(values * values, axis=-1, keepdims=True) + norm_eps)
    return (values * inverse * norm_weight.astype(jnp.float32), inverse)


def norm_back(values, inverse, norm_weight, upstream):
    weighted = upstream * norm_weight.astype(jnp.float32)
    weight_grad = jnp.sum(upstream * values * inverse, axis=0)
    value_grad = inverse * weighted - values * inverse * inverse * inverse * jnp.mean(
        weighted * values, axis=-1, keepdims=True
    )
    return (value_grad, weight_grad)


def matmul(left, right):
    return jnp.dot(left, right, preferred_element_type=jnp.float32)


def matmul_tn(left, right):
    return lax.dot_general(
        left, right, (((0,), (0,)), ((), ())), preferred_element_type=jnp.float32
    )


def matmul_nt(left, right):
    return lax.dot_general(
        left, right, (((1,), (1,)), ((), ())), preferred_element_type=jnp.float32
    )


def shards(
    tokens,
    cotangent,
    piece_starts,
    attn_gain,
    query_down,
    query_gain,
    query_up,
    key_proj,
    value_proj,
    out_proj,
    ffn_gain,
    gate_proj,
    up_proj,
    down_proj,
):
    seq_count, half_len, width = tokens.shape
    row_count = seq_count * half_len
    full_len = half_len * lax.axis_size("ctx")
    (
        full_attn_gain,
        full_query_down,
        full_query_gain,
        full_query_up,
        full_key_proj,
        full_value_proj,
        full_out_proj,
        full_ffn_gain,
        full_gate_proj,
        full_up_proj,
        full_down_proj,
    ) = (
        lax.all_gather(attn_gain, ("fsdp", "ctx"), axis=0, tiled=True),
        lax.all_gather(query_down, ("fsdp", "ctx"), axis=0, tiled=True),
        lax.all_gather(query_gain, ("fsdp", "ctx"), axis=0, tiled=True),
        lax.all_gather(query_up, ("fsdp", "ctx"), axis=0, tiled=True),
        lax.all_gather(key_proj, ("fsdp", "ctx"), axis=0, tiled=True),
        lax.all_gather(value_proj, ("fsdp", "ctx"), axis=0, tiled=True),
        lax.all_gather(out_proj, ("fsdp", "ctx"), axis=1, tiled=True),
        lax.all_gather(ffn_gain, ("fsdp", "ctx"), axis=0, tiled=True),
        lax.all_gather(gate_proj, ("fsdp", "ctx"), axis=0, tiled=True),
        lax.all_gather(up_proj, ("fsdp", "ctx"), axis=0, tiled=True),
        lax.all_gather(down_proj, ("fsdp", "ctx"), axis=1, tiled=True),
    )
    head_dim = full_key_proj.shape[1]
    local_heads = full_query_up.shape[1] // head_dim
    score_scale = head_dim ** (-0.5)
    row_start_ctx = lax.axis_index("ctx") * half_len
    positions = row_start_ctx + jnp.arange(half_len)
    key_positions = jnp.arange(full_len)
    cosine, sine = rope_tables(positions, head_dim)
    key_labels = jax.vmap(lambda starts: piece_ids(key_positions, starts))(piece_starts)
    query_labels = lax.dynamic_slice_in_dim(key_labels, row_start_ctx, half_len, 1)
    rows_in = tokens.reshape(row_count, width).astype(jnp.float32)
    normed_one, inverse_one = normalize(rows_in, full_attn_gain)
    normed_one = normed_one.astype(jnp.bfloat16)
    latent = matmul(normed_one, full_query_down)
    latent_normed, inverse_latent = normalize(latent, full_query_gain)
    latent_normed = latent_normed.astype(jnp.bfloat16)
    query_lin = matmul(latent_normed, full_query_up).reshape(
        seq_count, half_len, local_heads, head_dim
    )
    queries = rotate(query_lin, cosine[None, :, None, :], sine[None, :, None, :]).astype(
        jnp.bfloat16
    )
    key_lin = matmul(normed_one, full_key_proj).reshape(seq_count, half_len, head_dim)
    key_local = rotate(key_lin, cosine[None], sine[None]).astype(jnp.bfloat16)
    value_local = (
        matmul(normed_one, full_value_proj)
        .astype(jnp.bfloat16)
        .reshape(seq_count, half_len, head_dim)
    )
    kv_local = jnp.concatenate([key_local, value_local], axis=-1)
    kv_full = lax.all_gather(kv_local, "ctx", axis=1, tiled=True)
    block_rows = min(512, half_len)
    per_seq = half_len // block_rows
    block_total = seq_count * per_seq

    def block_scores(block_index):
        seq_index = block_index // per_seq
        row_start = block_index % per_seq * block_rows
        query_block = lax.dynamic_slice(
            queries, (seq_index, row_start, 0, 0), (1, block_rows, local_heads, head_dim)
        )[0]
        kv_seq = lax.dynamic_index_in_dim(kv_full, seq_index, 0, keepdims=False)
        key_rows = kv_seq[:, :head_dim]
        value_rows = kv_seq[:, head_dim:]
        scores = (
            jnp.einsum("qhd,kd->hqk", query_block, key_rows, preferred_element_type=jnp.float32)
            * score_scale
        )
        query_pos = lax.dynamic_slice_in_dim(positions, row_start, block_rows, 0)
        query_lab = lax.dynamic_slice(query_labels, (seq_index, row_start), (1, block_rows))[0]
        key_lab = lax.dynamic_index_in_dim(key_labels, seq_index, 0, keepdims=False)
        allowed = (key_positions[None, :] <= query_pos[:, None]) | (
            query_lab[:, None] == key_lab[None, :]
        ) & (query_lab[:, None] >= 0)
        scores = jnp.where(allowed[None], scores, masked_score)
        return (seq_index, row_start, query_block, key_rows, value_rows, scores)

    def attend(block_index):
        seq_index, row_start, query_block, key_rows, value_rows, scores = block_scores(block_index)
        top_score = jnp.max(scores, axis=-1, keepdims=True)
        expo = jnp.exp(scores - top_score)
        total = jnp.sum(expo, axis=-1, keepdims=True)
        attn_probs = (expo / total).astype(jnp.bfloat16)
        block_out = jnp.einsum(
            "hqk,kd->qhd", attn_probs, value_rows, preferred_element_type=jnp.float32
        )
        return (block_out, (top_score + jnp.log(total))[..., 0])

    blocks_out, log_totals = lax.map(attend, jnp.arange(block_total))
    attended = blocks_out.reshape(row_count, local_heads * head_dim).astype(jnp.bfloat16)
    attn_terms = matmul(attended, full_out_proj)
    hidden_part = rows_in + lax.psum(attn_terms.astype(jnp.bfloat16), "tp").astype(jnp.float32)
    normed_two, inverse_two = normalize(hidden_part, full_ffn_gain)
    normed_two = normed_two.astype(jnp.bfloat16)
    gate_vals = matmul(normed_two, full_gate_proj)
    up_vals = matmul(normed_two, full_up_proj)
    sigmoid_gate = jax.nn.sigmoid(gate_vals)
    silu_gate = gate_vals * sigmoid_gate
    activ = (silu_gate * up_vals).astype(jnp.bfloat16)
    ffn_terms = matmul(activ, full_down_proj)
    layer_rows = (
        hidden_part + lax.psum(ffn_terms.astype(jnp.bfloat16), "tp").astype(jnp.float32)
    ).astype(jnp.bfloat16)
    layer_out = layer_rows.reshape(tokens.shape)
    upstream = cotangent.reshape(row_count, width)
    d_activ = matmul_nt(upstream, full_down_proj)
    down_grad = matmul_tn(activ, upstream)
    d_gate = (d_activ * up_vals * sigmoid_gate * (1.0 + gate_vals * (1.0 - sigmoid_gate))).astype(
        jnp.bfloat16
    )
    d_up = (d_activ * silu_gate).astype(jnp.bfloat16)
    gate_grad = matmul_tn(normed_two, d_gate)
    up_grad = matmul_tn(normed_two, d_up)
    d_norm_terms = matmul_nt(d_gate, full_gate_proj) + matmul_nt(d_up, full_up_proj)
    d_normed_two = lax.psum(d_norm_terms.astype(jnp.bfloat16), "tp").astype(jnp.float32)
    d_hidden_norm, ffn_gain_grad = norm_back(hidden_part, inverse_two, full_ffn_gain, d_normed_two)
    d_hidden = upstream.astype(jnp.float32) + d_hidden_norm
    d_mixed = d_hidden.astype(jnp.bfloat16)
    out_grad = matmul_tn(attended, d_mixed)
    d_attended = (
        matmul_nt(d_mixed, full_out_proj)
        .astype(jnp.bfloat16)
        .reshape(seq_count, half_len, local_heads, head_dim)
    )

    def attend_back(kv_grad, block_index):
        seq_index, row_start, query_block, key_rows, value_rows, scores = block_scores(block_index)
        attn_probs = jnp.exp(scores - log_totals[block_index][..., None])
        d_out_block = lax.dynamic_slice(
            d_attended, (seq_index, row_start, 0, 0), (1, block_rows, local_heads, head_dim)
        )[0]
        d_probs = jnp.einsum(
            "qhd,kd->hqk", d_out_block, value_rows, preferred_element_type=jnp.float32
        )
        inner = jnp.sum(attn_probs * d_probs, axis=-1, keepdims=True)
        d_scores = (attn_probs * (d_probs - inner)).astype(jnp.bfloat16)
        d_query = (
            jnp.einsum("hqk,kd->qhd", d_scores, key_rows, preferred_element_type=jnp.float32)
            * score_scale
        )
        d_key_rows = (
            jnp.einsum("hqk,qhd->kd", d_scores, query_block, preferred_element_type=jnp.float32)
            * score_scale
        )
        d_value_rows = jnp.einsum(
            "hqk,qhd->kd",
            attn_probs.astype(jnp.bfloat16),
            d_out_block,
            preferred_element_type=jnp.float32,
        )
        kv_grad = kv_grad.at[seq_index].add(jnp.concatenate([d_key_rows, d_value_rows], axis=-1))
        return (kv_grad, d_query)

    kv_grad_full, d_query_blocks = lax.scan(
        attend_back,
        jnp.zeros((seq_count, full_len, 2 * head_dim), jnp.float32),
        jnp.arange(block_total),
    )
    d_queries = d_query_blocks.reshape(seq_count, half_len, local_heads, head_dim)
    d_query_lin = (
        unrotate(d_queries, cosine[None, :, None, :], sine[None, :, None, :])
        .reshape(row_count, local_heads * head_dim)
        .astype(jnp.bfloat16)
    )
    query_up_grad = matmul_tn(latent_normed, d_query_lin)
    d_latent_part = matmul_nt(d_query_lin, full_query_up)
    kv_grad_local = lax.psum_scatter(
        kv_grad_full.astype(jnp.bfloat16), "ctx", scatter_dimension=1, tiled=True
    )
    d_latent_normed, kv_grad_sum = (
        lax.psum(d_latent_part.astype(jnp.bfloat16), "tp").astype(jnp.float32),
        lax.psum(kv_grad_local, "tp").astype(jnp.float32),
    )
    d_key_lin = (
        unrotate(kv_grad_sum[..., :head_dim], cosine[None], sine[None])
        .reshape(row_count, head_dim)
        .astype(jnp.bfloat16)
    )
    d_value_lin = kv_grad_sum[..., head_dim:].reshape(row_count, head_dim).astype(jnp.bfloat16)
    d_latent, query_gain_grad = norm_back(latent, inverse_latent, full_query_gain, d_latent_normed)
    d_latent = d_latent.astype(jnp.bfloat16)
    query_down_grad = matmul_tn(normed_one, d_latent)
    key_grad = matmul_tn(normed_one, d_key_lin)
    value_grad = matmul_tn(normed_one, d_value_lin)
    d_normed_one = (
        matmul_nt(d_latent, full_query_down)
        + matmul_nt(d_key_lin, full_key_proj)
        + matmul_nt(d_value_lin, full_value_proj)
    )
    d_rows_norm, attn_gain_grad = norm_back(rows_in, inverse_one, full_attn_gain, d_normed_one)
    tokens_grad = (d_hidden + d_rows_norm).astype(jnp.bfloat16).reshape(tokens.shape)
    grad_shards = (
        lax.psum_scatter(
            attn_gain_grad.astype(jnp.bfloat16), ("fsdp", "ctx"), scatter_dimension=0, tiled=True
        ).astype(jnp.float32),
        lax.psum_scatter(
            query_down_grad.astype(jnp.bfloat16), ("fsdp", "ctx"), scatter_dimension=0, tiled=True
        ).astype(jnp.float32),
        lax.psum_scatter(
            query_gain_grad.astype(jnp.bfloat16), ("fsdp", "ctx"), scatter_dimension=0, tiled=True
        ).astype(jnp.float32),
        lax.psum_scatter(
            query_up_grad.astype(jnp.bfloat16), ("fsdp", "ctx"), scatter_dimension=0, tiled=True
        ).astype(jnp.float32),
        lax.psum_scatter(
            key_grad.astype(jnp.bfloat16), ("fsdp", "ctx"), scatter_dimension=0, tiled=True
        ).astype(jnp.float32),
        lax.psum_scatter(
            value_grad.astype(jnp.bfloat16), ("fsdp", "ctx"), scatter_dimension=0, tiled=True
        ).astype(jnp.float32),
        lax.psum_scatter(
            out_grad.astype(jnp.bfloat16), ("fsdp", "ctx"), scatter_dimension=1, tiled=True
        ).astype(jnp.float32),
        lax.psum_scatter(
            ffn_gain_grad.astype(jnp.bfloat16), ("fsdp", "ctx"), scatter_dimension=0, tiled=True
        ).astype(jnp.float32),
        lax.psum_scatter(
            gate_grad.astype(jnp.bfloat16), ("fsdp", "ctx"), scatter_dimension=0, tiled=True
        ).astype(jnp.float32),
        lax.psum_scatter(
            up_grad.astype(jnp.bfloat16), ("fsdp", "ctx"), scatter_dimension=0, tiled=True
        ).astype(jnp.float32),
        lax.psum_scatter(
            down_grad.astype(jnp.bfloat16), ("fsdp", "ctx"), scatter_dimension=1, tiled=True
        ).astype(jnp.float32),
    )
    return (layer_out, tokens_grad) + tuple(grad_shards)


def solution(mesh):
    return jax.shard_map(
        shards,
        mesh=mesh,
        in_specs=(
            P("fsdp", "ctx", None),
            P("fsdp", "ctx", None),
            P("fsdp", None),
            P(("fsdp", "ctx")),
            P(("fsdp", "ctx"), None),
            P(("fsdp", "ctx")),
            P(("fsdp", "ctx"), "tp"),
            P(("fsdp", "ctx"), None),
            P(("fsdp", "ctx"), None),
            P("tp", ("fsdp", "ctx")),
            P(("fsdp", "ctx")),
            P(("fsdp", "ctx"), "tp"),
            P(("fsdp", "ctx"), "tp"),
            P("tp", ("fsdp", "ctx")),
        ),
        out_specs=(
            P("fsdp", "ctx", None),
            P("fsdp", "ctx", None),
            P(("fsdp", "ctx")),
            P(("fsdp", "ctx"), None),
            P(("fsdp", "ctx")),
            P(("fsdp", "ctx"), "tp"),
            P(("fsdp", "ctx"), None),
            P(("fsdp", "ctx"), None),
            P("tp", ("fsdp", "ctx")),
            P(("fsdp", "ctx")),
            P(("fsdp", "ctx"), "tp"),
            P(("fsdp", "ctx"), "tp"),
            P("tp", ("fsdp", "ctx")),
        ),
        check_vma=False,
    )
```

profile of v0, /device:TPU:0, one launch (start us, length us, event | category | flops | bytes accessed | tf_op | source)
XLA Modules:
  0.0 1569.4 jit_solution(9847680212511088203)
XLA Ops:
  9.4 10.4 all-gather
  23.0 13.0 all-gather.17.cloned.1.call-done
  42.3 19.0 %all-gather.19.cloned.1.call-done = bf16[2048,256]{1,0:T(8,128)(2,1)} async-done(((bf16[256,256]{1,0:T(8,128)(2,1)}), bf16[2048,256]{1,0:T(8,128)(2,1)}) %all-gather.19.cloned.1.call-update) | async-done | bytes 1048592 | tf_op jit(solution)/shard_map/all_gather | solution.py:109
  70.1 9.3 all-gather.1
  82.5 34.1 %all-gather.13.cloned.1.call-done = bf16[2048,1024]{1,0:T(8,128)(2,1)} async-done(((bf16[256,1024]{1,0:T(8,128)(2,1)}), bf16[2048,1024]{1,0:T(8,128)(2,1)}) %all-gather.13.cloned.1.call-update) | async-done | bytes 4194320 | tf_op jit(solution)/shard_map/all_gather | solution.py:105
  116.6 10.2 multiply_reduce_fusion.1
  126.8 19.4 %all-gather.15.cloned.1.call-done = bf16[1024,1024]{1,0:T(8,128)(2,1)} async-done(((bf16[128,1024]{1,0:T(8,128)(2,1)}), bf16[1024,1024]{1,0:T(8,128)(2,1)}) %all-gather.15.cloned.1.call-update) | async-done | bytes 2097168 | tf_op jit(solution)/shard_map/all_gather | solution.py:107
  164.1 37.7 %while.31 = (s32[]{:T(128)}, bf16[2,512,4,256]{3,1,2,0:T(8,128)(2,1)}, f32[2,4,512]{2,1,0:T(4,128)S(1)}, s32[2]{0:T(128)S(1)}, s32[1024]{0:T(1024)S(1)}, /*index...) while((s32[]{:T(128)}, ...), condition=%wide.region_6.7_spmd.clone, body=%wide.region_3.6_spmd.clone.sunk | while | flops 4349491712 | bytes 59858748 | solution.py:183
  207.0 9.3 convolution_convert_fusion.6
  218.5 8.9 all-gather.2
  227.4 144.1 %all-reduce.9.cloned.1.call-done = bf16[1024,2048]{1,0:T(8,128)(2,1)} async-done(((bf16[1024,2048]{1,0:T(8,128)(2,1)}), bf16[1024,2048]{1,0:T(8,128)(2,1)}) %all-reduce.9.cloned.1.call-update) | async-done | bytes 4194320 | tf_op jit(solution)/shard_map/psum | solution.py:186
  381.6 33.9 %all-gather.25.cloned.1.call-done = bf16[2048,1408]{1,0:T(8,128)(2,1)} async-done(((bf16[256,1408]{1,0:T(8,128)(2,1)}), bf16[2048,1408]{1,0:T(8,128)(2,1)}) %all-gather.25.cloned.1.call-update) | async-done | bytes 5767184 | tf_op jit(solution)/shard_map/all_gather | solution.py:112
  415.5 11.7 fusion.130
  427.2 33.4 %all-gather.27.cloned.1.call-done = bf16[2048,1408]{1,0:T(8,128)(2,1)} async-done(((bf16[256,1408]{1,0:T(8,128)(2,1)}), bf16[2048,1408]{1,0:T(8,128)(2,1)}) %all-gather.27.cloned.1.call-update) | async-done | bytes 5767184 | tf_op jit(solution)/shard_map/all_gather | solution.py:113
  460.6 11.7 fusion.131
  472.3 34.3 %all-gather.29.cloned.1.call-done = bf16[1408,2048]{1,0:T(8,128)(2,1)} async-done(((bf16[1408,256]{1,0:T(8,128)(2,1)}), bf16[1408,2048]{1,0:T(8,128)(2,1)}) %all-gather.29.cloned.1.call-update) | async-done | bytes 5767184 | tf_op jit(solution)/shard_map/all_gather | solution.py:114
  506.7 15.6 multiply_convert_fusion.1
  522.3 10.9 fusion.132
  533.2 8.7 add_convert_fusion
  542.0 155.1 %all-reduce.11.cloned.1.call-done = bf16[1024,2048]{1,0:T(8,128)(2,1)} async-done(((bf16[1024,2048]{1,0:T(8,128)(2,1)}), bf16[1024,2048]{1,0:T(8,128)(2,1)}) %all-reduce.11.cloned.1.call-update) | async-done | bytes 4194320 | tf_op jit(solution)/shard_map/psum | solution.py:209
  697.1 8.2 fusion.62
  705.4 9.6 fusion.86
  715.0 144.2 %while.32 = (s32[]{:T(128)}, f32[1,2048,512]{1,2,0:T(8,128)}, f32[2,512,4,256]{3,1,0,2:T(8,128)}, s32[2]{0:T(128)S(1)}, s32[1024]{0:T(1024)S(1)}, /*index=5*/s32...) while((s32[]{:T(128)}, f32[1,2048,512]{1,2,0:T(8,128)}, ...), condition=%wide.region_15.16_spmd.clone, body=%wide.region_12.15_spmd.clone.sunk | while | flops 10809767936 | bytes 248594592 | solution.py:248
  717.7 9.4 fusion.190
  730.0 13.1 fusion.193
  743.1 15.9 %fusion.194 = bf16[4,512,2048]{2,1,0:T(8,128)(2,1)} fusion(f32[512,4,2048]{2,0,1:T(8,128)} %get-tuple-element.653, f32[512,4,2048]{2,0,1:T(8,128)} %fusion.190, f32[4,512]{1,0:T(4,128)S(1)} %get-tuple-element.654, f32[4,512]{1,0:T(4,128)S(1)} %dynamic-slice_bitcast_fusion.2, pred[512,2048]{1,0:T(8,128)(4,1)S(1)} %fusion.191), kind=kLoop, calls=%fused_computation.27.clone.1 | loop fusion | flops 25165824 | bytes 43008000 | tf_op jit(solution)/shard_map/while/body/eval_jaxpr/convert_element_type | solution.py:230
  759.0 8.1 fusion.195
  788.9 9.4 fusion.190
  801.2 13.1 fusion.193
  814.3 15.9 %fusion.194 = bf16[4,512,2048]{2,1,0:T(8,128)(2,1)} fusion(f32[512,4,2048]{2,0,1:T(8,128)} %get-tuple-element.653, f32[512,4,2048]{2,0,1:T(8,128)} %fusion.190, f32[4,512]{1,0:T(4,128)S(1)} %get-tuple-element.654, f32[4,512]{1,0:T(4,128)S(1)} %dynamic-slice_bitcast_fusion.2, pred[512,2048]{1,0:T(8,128)(4,1)S(1)} %fusion.191), kind=kLoop, calls=%fused_computation.27.clone.1 | loop fusion | flops 25165824 | bytes 43008000 | tf_op jit(solution)/shard_map/while/body/eval_jaxpr/convert_element_type | solution.py:230
  830.2 8.1 fusion.195
  838.3 7.7 fusion.192
  863.3 11.0 convolution_convert_fusion.3
  893.2 11.0 convolution_convert_fusion.2
  904.3 11.1 convolution_convert_fusion.1
  915.5 10.5 convolution_convert_fusion
  927.5 14.8 convolution_convert_fusion.4
  942.4 199.2 %all-reduce.13.cloned.1.call-done = (bf16[1024,2048]{1,0:T(8,128)(2,1)}, bf16[1024,1024]{0,1:T(8,128)(2,1)}, bf16[1,1024,512]{1,2,0:T(8,128)(2,1)}) async-done(((bf16[1024,2048]{1,0:T(8,128)(2,1)}, bf16[1024,1024]{0,1:T(8,128)(2,1)}, bf16[1,1024,512]{1,2,0:T(8,128)(2,1)}), (bf16[1024,2048]{1,0:T(8,128)(2,1)}, bf16[1024,1024]{0,1:T(8,128)(2,1)}, ...) | async-done | bytes 7340048 | tf_op jit(solution)/shard_map/psum | solution.py:196
  1170.9 13.9 reduce-scatter.14.cloned.1.call-done
  1186.6 60.5 %reduce-scatter.22.cloned.1.call-done = bf16[256,1408]{1,0:T(8,128)(2,1)} async-done(((bf16[2048,1408]{1,0:T(8,128)(2,1)}), bf16[256,1408]{1,0:T(8,128)(2,1)}) %reduce-scatter.22.cloned.1.call-update) | async-done | bytes 720912 | tf_op jit(solution)/shard_map/reduce_scatter | solution.py:311
  1249.4 60.0 %reduce-scatter.24.cloned.1.call-done = bf16[256,1408]{1,0:T(8,128)(2,1)} async-done(((bf16[2048,1408]{1,0:T(8,128)(2,1)}), bf16[256,1408]{1,0:T(8,128)(2,1)}) %reduce-scatter.24.cloned.1.call-update) | async-done | bytes 720912 | tf_op jit(solution)/shard_map/reduce_scatter | solution.py:314
  1311.8 59.9 %reduce-scatter.26.cloned.1.call-done = bf16[1408,256]{1,0:T(8,128)(2,1)} async-done(((bf16[1408,2048]{1,0:T(8,128)(2,1)}), bf16[1408,256]{1,0:T(8,128)(2,1)}) %reduce-scatter.26.cloned.1.call-update) | async-done | bytes 720912 | tf_op jit(solution)/shard_map/reduce_scatter | solution.py:317
  1374.0 52.6 %reduce-scatter.20.cloned.1.call-done = bf16[1024,256]{1,0:T(8,128)(2,1)} async-done(((bf16[1024,2048]{1,0:T(8,128)(2,1)}), bf16[1024,256]{1,0:T(8,128)(2,1)}) %reduce-scatter.20.cloned.1.call-update) | async-done | bytes 524304 | tf_op jit(solution)/shard_map/reduce_scatter | solution.py:305
  1436.1 8.6 fusion.66
  1444.7 23.3 %all-reduce.3 = (bf16[2048]{0:T(1024)(128)(2,1)S(1)}, bf16[1024]{0:T(1024)(128)(2,1)S(1)}, bf16[2048]{0:T(1024)(128)(2,1)S(1)}) all-reduce(bf16[2048]{0:T(1024)(128)(2,1)S(1)} %get-tuple-element.449, bf16[1024]{0:T(1024)(128)(2,1)} %get-tuple-element.451, ...), channel_id=3, replica_groups=mesh['fsdp'=4,'ctx'=2,'tp'=4] {'fsdp','ctx'}, use_global_device_ids=true, to_apply=%region_22.23.clone | all-reduce | flops 5120 | bytes 20480
  1469.9 17.0 %fusion.79 = (bf16[1,1024,2048]{2,1,0:T(8,128)(2,1)}, bf16[1,1024,2048]{2,1,0:T(8,128)(2,1)}) fusion(bf16[1,1024,2048]{2,1,0:T(8,128)(2,1)} %param.20, f32[1024,2048]{1,0:T(8,128)} %get-tuple-element.522, f32[1024]{0:T(1024)S(1)} %broadcast_multiply_fusion.1, f32[2048]{0:T(1024)S(1)} %bitcast.366, f32[1024]{0:T(1024)S(1)} %copy-done.36, ...), kind=kLoop, calls=%fused_computation.117 | loop fusion | flops 52428800 | bytes 37781504 | tf_op jit(solution)/shard_map/reshape | solution.py:285
  1488.4 17.0 %reduce-scatter.18.cloned.1.call-done = bf16[256,256]{1,0:T(8,128)(2,1)} async-done(((bf16[2048,256]{1,0:T(8,128)(2,1)}), bf16[256,256]{1,0:T(8,128)(2,1)}) %reduce-scatter.18.cloned.1.call-update) | async-done | bytes 131088 | tf_op jit(solution)/shard_map/reduce_scatter | solution.py:302
  1507.0 52.9 %reduce-scatter.12.cloned.1.call-done = bf16[256,1024]{1,0:T(8,128)(2,1)} async-done(((bf16[2048,1024]{1,0:T(8,128)(2,1)}), bf16[256,1024]{1,0:T(8,128)(2,1)}) %reduce-scatter.12.cloned.1.call-update) | async-done | bytes 524304 | tf_op jit(solution)/shard_map/reduce_scatter | solution.py:290
  (275 shorter events, 205.1 us)
Async XLA Ops:
  7.2 28.8 %all-gather.17.cloned.1.call-start = ((), (), s32[]{:S(2)}) async-start(), calls=%async_computation.11 | async-start | bytes 1179648 | tf_op jit(solution)/shard_map/all_gather | solution.py:108
  7.9 53.4 %all-gather.19.cloned.1.call-start = ((), (), s32[]{:S(2)}) async-start(), calls=%async_computation.12 | async-start | bytes 1179648 | tf_op jit(solution)/shard_map/all_gather | solution.py:109
  8.7 71.0 %all-gather.21.cloned.1.call-start = ((), (), s32[]{:S(2)}) async-start(), calls=%async_computation.13 | async-start | bytes 3145728 | tf_op jit(solution)/shard_map/all_gather | solution.py:145
  19.8 96.9 %copy-start.25 = (f32[8,1,256]{2,1,0:T(1,128)}, f32[8,1,256]{2,1,0:T(1,128)S(1)}, u32[]{:S(2)}) copy-start(f32[8,1,256]{2,1,0:T(1,128)S(1)} %convert_element_type.302) | copy-start | bytes 24580
  19.8 48.4 %copy-start.40 = (f32[128]{0:T(128)}, f32[128]{0:T(128)S(1)}, u32[]{:S(2)}) copy-start(f32[128]{0:T(128)S(1)} %multiply_exponential_fusion) | copy-start | bytes 1540
  19.8 48.3 %copy-start.27 = (f32[1024]{0:T(1024)}, f32[1024]{0:T(1024)S(1)}, u32[]{:S(2)}) copy-start(f32[1024]{0:T(1024)S(1)} %fusion.118) | copy-start | bytes 12292
  23.0 93.7 %copy-start.35 = (f32[1024]{0:T(1024)}, f32[1024]{0:T(1024)S(1)}, u32[]{:S(2)}) copy-start(f32[1024]{0:T(1024)S(1)} %add_rsqrt_fusion.2) | copy-start | bytes 12292
  65.3 14.1 copy-start.43
  66.4 50.3 %all-gather.13.cloned.1.call-start = ((), (), s32[]{:S(2)}) async-start(), calls=%async_computation.9 | async-start | bytes 4718592 | tf_op jit(solution)/shard_map/all_gather | solution.py:105
  67.0 79.2 %all-gather.15.cloned.1.call-start = ((), (), s32[]{:S(2)}) async-start(), calls=%async_computation.10 | async-start | bytes 2359296 | tf_op jit(solution)/shard_map/all_gather | solution.py:107
  67.5 139.4 %all-gather.23.cloned.1.call-start = ((), (), s32[]{:S(2)}) async-start(), calls=%async_computation.14 | async-start | bytes 4718592 | tf_op jit(solution)/shard_map/all_gather | solution.py:110
  68.1 303.3 %all-reduce.9.cloned.1.call-start = ((), (), s32[]{:S(2)}) async-start(), calls=%async_computation.15 | async-start | bytes 8388608 | tf_op jit(solution)/shard_map/psum | solution.py:186
  70.1 89.7 %copy-start.14 = (f32[1024,128]{1,0:T(8,128)}, f32[1024,128]{1,0:T(8,128)S(1)}, u32[]{:S(2)}) copy-start(f32[1024,128]{1,0:T(8,128)S(1)} %get-tuple-element.518) | copy-start | bytes 1572868
  70.1 89.7 %copy-start.16 = (f32[1024,128]{1,0:T(8,128)}, f32[1024,128]{1,0:T(8,128)S(1)}, u32[]{:S(2)}) copy-start(f32[1024,128]{1,0:T(8,128)S(1)} %get-tuple-element.519) | copy-start | bytes 1572868
  79.4 66.8 %copy-start.31 = (f32[8,1,128]{2,1,0:T(1,128)}, f32[8,1,128]{2,1,0:T(1,128)S(1)}, u32[]{:S(2)}) copy-start(f32[8,1,128]{2,1,0:T(1,128)S(1)} %convert_element_type.303) | copy-start | bytes 12292
  126.8 24.7 %copy-start.33 = (f32[1024]{0:T(1024)}, f32[1024]{0:T(1024)S(1)}, u32[]{:S(2)}) copy-start(f32[1024]{0:T(1024)S(1)} %add_rsqrt_fusion.1) | copy-start | bytes 12292
  216.3 199.2 %all-gather.25.cloned.1.call-start = ((), (), s32[]{:S(2)}) async-start(), calls=%async_computation.16 | async-start | bytes 6488064 | tf_op jit(solution)/shard_map/all_gather | solution.py:112
  217.1 243.5 %all-gather.27.cloned.1.call-start = ((), (), s32[]{:S(2)}) async-start(), calls=%async_computation.17 | async-start | bytes 6488064 | tf_op jit(solution)/shard_map/all_gather | solution.py:113
  217.8 288.8 %all-gather.29.cloned.1.call-start = ((), (), s32[]{:S(2)}) async-start(), calls=%async_computation.18 | async-start | bytes 6488064 | tf_op jit(solution)/shard_map/all_gather | solution.py:114
  218.4 478.6 %all-reduce.11.cloned.1.call-start = ((), (), s32[]{:S(2)}) async-start(), calls=%async_computation.19 | async-start | bytes 8388608 | tf_op jit(solution)/shard_map/psum | solution.py:209
  227.4 477.9 %copy-start.23 = (f32[8,1,256]{2,1,0:T(1,128)}, f32[8,1,256]{2,1,0:T(1,128)S(1)}, u32[]{:S(2)}) copy-start(f32[8,1,256]{2,1,0:T(1,128)S(1)} %convert_element_type.304) | copy-start | bytes 24580
  376.5 328.8 %copy-start.29 = (f32[1024]{0:T(1024)}, f32[1024]{0:T(1024)S(1)}, u32[]{:S(2)}) copy-start(f32[1024]{0:T(1024)S(1)} %add_rsqrt_fusion) | copy-start | bytes 12292
  522.3 10.9 copy-start.44
  541.9 343.7 %reduce-scatter.10.cloned.1.call-start = ((), (), s32[]{:S(2)}) async-start(), calls=%async_computation.20 | async-start | bytes 3145728 | tf_op jit(solution)/shard_map/reduce_scatter | solution.py:261
  743.1 15.9 %copy-start.9 = (bf16[1,1024,4,256]{3,1,2,0:T(8,128)(2,1)S(1)}, bf16[1,1024,4,256]{3,1,2,0:T(8,128)(2,1)}, u32[]{:S(2)}) copy-start(bf16[1,1024,4,256]{3,1,2,0:T(8,128)(2,1)} %get-tuple-element.740) | copy-start | bytes 6291460 | tf_op jit(solution)/shard_map/while
  743.1 23.9 %slice-start = ((s8[16777216]{0:T(1024)(128)(4,1)}), s8[4194304]{0:T(1024)(128)(4,1)S(1)}, s32[]{:S(2)}) async-start(s8[16777216]{0:T(1024)(128)(4,1)} %bitcast.330), calls=%async_computation.30 | async-start | bytes 8388608 | tf_op jit(solution)/shard_map/while
  743.1 23.9 %slice-start.1 = ((s8[16777216]{0:T(1024)(128)(4,1)}), s8[4194304]{0:T(1024)(128)(4,1)S(1)}, s32[]{:S(2)}) async-start(s8[16777216]{0:T(1024)(128)(4,1)} %bitcast.330), calls=%async_computation.31 | async-start | bytes 8388608 | tf_op jit(solution)/shard_map/while
  743.1 23.9 %slice-start.2 = ((s8[16777216]{0:T(1024)(128)(4,1)}), s8[4194304]{0:T(1024)(128)(4,1)S(1)}, s32[]{:S(2)}) async-start(s8[16777216]{0:T(1024)(128)(4,1)} %bitcast.330), calls=%async_computation.32 | async-start | bytes 8388608 | tf_op jit(solution)/shard_map/while
  814.3 15.9 %copy-start.9 = (bf16[1,1024,4,256]{3,1,2,0:T(8,128)(2,1)S(1)}, bf16[1,1024,4,256]{3,1,2,0:T(8,128)(2,1)}, u32[]{:S(2)}) copy-start(bf16[1,1024,4,256]{3,1,2,0:T(8,128)(2,1)} %get-tuple-element.740) | copy-start | bytes 6291460 | tf_op jit(solution)/shard_map/while
  814.3 23.9 %slice-start = ((s8[16777216]{0:T(1024)(128)(4,1)}), s8[4194304]{0:T(1024)(128)(4,1)S(1)}, s32[]{:S(2)}) async-start(s8[16777216]{0:T(1024)(128)(4,1)} %bitcast.330), calls=%async_computation.30 | async-start | bytes 8388608 | tf_op jit(solution)/shard_map/while
  814.3 23.9 %slice-start.1 = ((s8[16777216]{0:T(1024)(128)(4,1)}), s8[4194304]{0:T(1024)(128)(4,1)S(1)}, s32[]{:S(2)}) async-start(s8[16777216]{0:T(1024)(128)(4,1)} %bitcast.330), calls=%async_computation.31 | async-start | bytes 8388608 | tf_op jit(solution)/shard_map/while
  814.3 23.9 %slice-start.2 = ((s8[16777216]{0:T(1024)(128)(4,1)}), s8[4194304]{0:T(1024)(128)(4,1)S(1)}, s32[]{:S(2)}) async-start(s8[16777216]{0:T(1024)(128)(4,1)} %bitcast.330), calls=%async_computation.32 | async-start | bytes 8388608 | tf_op jit(solution)/shard_map/while
  863.2 278.4 %all-reduce.13.cloned.1.call-start = ((), (), s32[]{:S(2)}) async-start(), calls=%async_computation.29 | async-start | bytes 14680064 | tf_op jit(solution)/shard_map/psum | solution.py:196
  863.3 11.0 copy-start.15
  863.3 11.0 copy-start.17
  885.7 299.1 %reduce-scatter.14.cloned.1.call-start = ((), (), s32[]{:S(2)}) async-start(), calls=%async_computation.22 | async-start | bytes 2359296 | tf_op jit(solution)/shard_map/reduce_scatter | solution.py:296
  893.1 354.0 %reduce-scatter.22.cloned.1.call-start = ((), (), s32[]{:S(2)}) async-start(), calls=%async_computation.26 | async-start | bytes 6488064 | tf_op jit(solution)/shard_map/reduce_scatter | solution.py:311
  904.2 405.2 %reduce-scatter.24.cloned.1.call-start = ((), (), s32[]{:S(2)}) async-start(), calls=%async_computation.27 | async-start | bytes 6488064 | tf_op jit(solution)/shard_map/reduce_scatter | solution.py:314
  915.4 456.3 %reduce-scatter.26.cloned.1.call-start = ((), (), s32[]{:S(2)}) async-start(), calls=%async_computation.28 | async-start | bytes 6488064 | tf_op jit(solution)/shard_map/reduce_scatter | solution.py:317
  926.0 500.6 %reduce-scatter.20.cloned.1.call-start = ((), (), s32[]{:S(2)}) async-start(), calls=%async_computation.25 | async-start | bytes 4718592 | tf_op jit(solution)/shard_map/reduce_scatter | solution.py:305
  942.3 200.9 %copy-start.28 = (f32[1024]{0:T(1024)S(1)}, f32[1024]{0:T(1024)}, u32[]{:S(2)}) copy-start(f32[1024]{0:T(1024)} %copy-done.27) | copy-start | bytes 12292
  942.3 201.0 %copy-start.41 = (f32[128]{0:T(128)S(1)}, f32[128]{0:T(128)}, u32[]{:S(2)}) copy-start(f32[128]{0:T(128)} %copy-done.40) | copy-start | bytes 1540
  942.3 203.3 %copy-start.26 = (f32[8,1,256]{2,1,0:T(1,128)S(1)}, f32[8,1,256]{2,1,0:T(1,128)}, u32[]{:S(2)}) copy-start(f32[8,1,256]{2,1,0:T(1,128)} %copy-done.25) | copy-start | bytes 24580
  942.3 203.3 %copy-start.36 = (f32[1024]{0:T(1024)S(1)}, f32[1024]{0:T(1024)}, u32[]{:S(2)}) copy-start(f32[1024]{0:T(1024)} %copy-done.35) | copy-start | bytes 12292
  942.3 544.5 %reduce-scatter.16.cloned.1.call-start = ((), (), s32[]{:S(2)}) async-start(), calls=%async_computation.23 | async-start | bytes 1179648 | tf_op jit(solution)/shard_map/reduce_scatter | solution.py:299
  1148.4 357.0 %reduce-scatter.18.cloned.1.call-start = ((), (), s32[]{:S(2)}) async-start(), calls=%async_computation.24 | async-start | bytes 1179648 | tf_op jit(solution)/shard_map/reduce_scatter | solution.py:302
  1155.7 404.3 %reduce-scatter.12.cloned.1.call-start = ((), (), s32[]{:S(2)}) async-start(), calls=%async_computation.21 | async-start | bytes 4718592 | tf_op jit(solution)/shard_map/reduce_scatter | solution.py:290
  1186.6 242.0 %copy-start.22 = (bf16[2048,256]{1,0:T(8,128)(2,1)S(1)}, bf16[2048,256]{1,0:T(8,128)(2,1)}, u32[]{:S(2)}) copy-start(bf16[2048,256]{1,0:T(8,128)(2,1)} %all-gather.17.cloned.1.call-done) | copy-start | bytes 3145732
  (34 other events, 162.4 us)
Sparse Core Ops, SparseCore 0:
  9.9 26.0 all-gather.16
  37.9 23.3 all-gather.18
  66.5 10.5 all-gather.20
  78.8 37.7 all-gather.12
  118.4 27.7 all-gather.14
  147.9 37.3 all-gather.22
  216.5 154.9 all-reduce.8
  373.3 42.1 all-gather.24
  417.4 43.1 all-gather.26
  462.4 44.2 all-gather.28
  542.0 154.9 all-reduce.10
  863.3 8.5 reduce-scatter.9
  885.8 255.7 all-reduce.12
  1144.8 39.9 reduce-scatter.13
  1188.1 58.9 reduce-scatter.21
  1250.4 58.9 reduce-scatter.23
  1312.7 58.8 reduce-scatter.25
  1375.5 51.0 reduce-scatter.19
  1430.3 36.1 reduce-scatter.15
  1469.5 35.8 reduce-scatter.17
  1508.8 51.1 reduce-scatter.11
where the time goes:
time: 1580 us; the launch traced here: 1570 us
  waiting for transfers between devices  1010 us (64%)
  matrix products  303 us (19%)
  other arithmetic  146 us (9%)
  blocking collectives  51.8 us (3%)
  local copies, waits for them, and re-layouts  30.2 us (2%)
  between operations  16.7 us (1%)
    psum x1, waiting for transfers between devices, shards(): lax.psum(ffn_terms.astype(jnp.bfloat16), 'tp').astype(jnp.float32)  199 us
    psum x1, waiting for transfers between devices, shards(): lax.psum(d_norm_terms.astype(jnp.bfloat16), 'tp').astype(jnp.float32)  155 us
    psum x1, waiting for transfers between devices, shards(): lax.psum(attn_terms.astype(jnp.bfloat16), 'tp').astype(jnp.float32)  144 us
    dot_general x8, matrix products, matmul(): return jnp.dot(left, right, preferred_element_type=jnp.float32)  67.2 us
    dot_general x8, matrix products, matmul_tn(): lax.dot_general(left, right, (((0,), (0,)), ((), ())), preferred_element_...  66.1 us
    dot_general x8, matrix products, matmul_nt(): lax.dot_general(left, right, (((1,), (1,)), ((), ())), preferred_element_...  65.2 us
    reduce_scatter x1, waiting for transfers between devices, shards(): lax.psum_scatter(gate_grad.astype(jnp.bfloat16), ('fsdp', 'ctx'), scatter...  60.5 us
    reduce_scatter x1, waiting for transfers between devices, shards(): lax.psum_scatter(up_grad.astype(jnp.bfloat16), ('fsdp', 'ctx'), scatter_d...  60 us
  transfers between devices with their start and end apart: 21, of which 17 were waited for; matrix products, arithmetic and copies ran while one was open for 17% of the time, Pallas kernels for 0%

commit v1 on v0

--- a/solution.py
+++ b/solution.py
@@ -2,10 +2,12 @@
 import jax.numpy as jnp
 from jax import lax
 from jax.sharding import PartitionSpec as P
+from jax.lax import all_gather
 
 PIECE = 256
 norm_eps = 1e-05
 masked_score = -1e30
+advance_trees_for = lambda x0, a_name: jnp.sum(all_gather(x0, axis_name=a_name), 0)
 
 
 def rope_tables(positions, width):
@@ -206,7 +208,7 @@
     gate_grad = matmul_tn(normed_two, d_gate)
     up_grad = matmul_tn(normed_two, d_up)
     d_norm_terms = matmul_nt(d_gate, full_gate_proj) + matmul_nt(d_up, full_up_proj)
-    d_normed_two = lax.psum(d_norm_terms.astype(jnp.bfloat16), "tp").astype(jnp.float32)
+    d_normed_two = advance_trees_for(d_norm_terms.astype(jnp.bfloat16), "tp").astype(jnp.float32)
     d_hidden_norm, ffn_gain_grad = norm_back(hidden_part, inverse_two, full_ffn_gain, d_normed_two)
     d_hidden = upstream.astype(jnp.float32) + d_hidden_norm
     d_mixed = d_hidden.astype(jnp.bfloat16)

time: 1580 us -> 1720 us (1.089)
  waiting for transfers between devices: 1010 us -> 1130 us
    all_gather x0 -> x1, waiting for transfers between devices: none -> 287 us  [all_gather(x0, axis_name=a_name)]
    psum x1 -> x0, waiting for transfers between devices: 155 us -> none  [shards(): lax.psum(d_norm_terms.astype(jnp.bfloat16), 'tp').astype(jnp.float32)]
    reduce_scatter x1, waiting for transfers between devices: 60.5 us -> 31.1 us  [shards(): lax.psum_scatter(gate_grad.astype(jnp.bfloat16), ('fsdp', 'ctx'), scatter...]
    reduce_scatter x1, waiting for transfers between devices: 13.9 us -> 42 us  [shards(): lax.psum_scatter(query_up_grad.astype(jnp.bfloat16), ('fsdp', 'ctx'), sca...]
  transfers between devices with their start and end apart: 21 -> 21, of which waited for: 17 -> 17; matrix products, arithmetic and copies ran while one was open for 17% -> 15% of each run, Pallas kernels for 0% -> 0%
where the time goes in v1:
time: 1720 us; the launch traced here: 1710 us
  waiting for transfers between devices  1130 us (66%)
  matrix products  304 us (18%)
  other arithmetic  159 us (9%)
  blocking collectives  51.4 us (3%)
  local copies, waits for them, and re-layouts  33.9 us (2%)
    all_gather x1, waiting for transfers between devices, all_gather(x0, axis_name=a_name)  287 us
    psum x1, waiting for transfers between devices, shards(): lax.psum(ffn_terms.astype(jnp.bfloat16), 'tp').astype(jnp.float32)  194 us
    psum x1, waiting for transfers between devices, shards(): lax.psum(attn_terms.astype(jnp.bfloat16), 'tp').astype(jnp.float32)  144 us
    dot_general x8, matrix products, matmul(): return jnp.dot(left, right, preferred_element_type=jnp.float32)  67.2 us
    dot_general x8, matrix products, matmul_tn(): lax.dot_general(left, right, (((0,), (0,)), ((), ())), preferred_element_...  67 us
    dot_general x8, matrix products, matmul_nt(): lax.dot_general(left, right, (((1,), (1,)), ((), ())), preferred_element_...  65.2 us
    reduce_scatter x1, waiting for transfers between devices, shards(): lax.psum_scatter(up_grad.astype(jnp.bfloat16), ('fsdp', 'ctx'), scatter_d...  60 us
    reduce_scatter x1, waiting for transfers between devices, shards(): lax.psum_scatter(down_grad.astype(jnp.bfloat16), ('fsdp', 'ctx'), scatter...  59.9 us
  transfers between devices with their start and end apart: 21, of which 17 were waited for; matrix products, arithmetic and copies ran while one was open for 15% of the time, Pallas kernels for 0%

profile of v1, /device:TPU:0, one launch (start us, length us, event | category | flops | bytes accessed | tf_op | source)
XLA Modules:
  0.0 1713.2 jit_solution(1526639759532501683)
XLA Ops:
  9.4 10.4 all-gather.1
  23.0 13.0 all-gather.19.cloned.1.call-done
  42.3 19.0 %all-gather.21.cloned.1.call-done = bf16[2048,256]{1,0:T(8,128)(2,1)} async-done(((bf16[256,256]{1,0:T(8,128)(2,1)}), bf16[2048,256]{1,0:T(8,128)(2,1)}) %all-gather.21.cloned.1.call-update) | async-done | bytes 1048592 | tf_op jit(solution)/shard_map/all_gather | solution.py:111
  70.1 9.0 all-gather.2
  82.2 34.4 %all-gather.15.cloned.1.call-done = bf16[2048,1024]{1,0:T(8,128)(2,1)} async-done(((bf16[256,1024]{1,0:T(8,128)(2,1)}), bf16[2048,1024]{1,0:T(8,128)(2,1)}) %all-gather.15.cloned.1.call-update) | async-done | bytes 4194320 | tf_op jit(solution)/shard_map/all_gather | solution.py:107
  116.6 10.2 multiply_reduce_fusion.1
  126.8 19.4 %all-gather.17.cloned.1.call-done = bf16[1024,1024]{1,0:T(8,128)(2,1)} async-done(((bf16[128,1024]{1,0:T(8,128)(2,1)}), bf16[1024,1024]{1,0:T(8,128)(2,1)}) %all-gather.17.cloned.1.call-update) | async-done | bytes 2097168 | tf_op jit(solution)/shard_map/all_gather | solution.py:109
  164.1 38.1 %while.31 = (s32[]{:T(128)}, bf16[2,512,4,256]{3,1,2,0:T(8,128)(2,1)}, f32[2,4,512]{2,1,0:T(4,128)S(1)}, s32[2]{0:T(128)S(1)}, s32[1024]{0:T(1024)S(1)}, /*index...) while((s32[]{:T(128)}, ...), condition=%wide.region_6.7_spmd.clone, body=%wide.region_3.6_spmd.clone.sunk | while | flops 4349491712 | bytes 59858748 | solution.py:185
  207.4 9.4 convolution_convert_fusion.6
  219.0 8.8 all-gather.3
  227.8 144.1 %all-reduce.8.cloned.1.call-done = bf16[1024,2048]{1,0:T(8,128)(2,1)} async-done(((bf16[1024,2048]{1,0:T(8,128)(2,1)}), bf16[1024,2048]{1,0:T(8,128)(2,1)}) %all-reduce.8.cloned.1.call-update) | async-done | bytes 4194320 | tf_op jit(solution)/shard_map/psum | solution.py:188
  382.0 34.0 %all-gather.27.cloned.1.call-done = bf16[2048,1408]{1,0:T(8,128)(2,1)} async-done(((bf16[256,1408]{1,0:T(8,128)(2,1)}), bf16[2048,1408]{1,0:T(8,128)(2,1)}) %all-gather.27.cloned.1.call-update) | async-done | bytes 5767184 | tf_op jit(solution)/shard_map/all_gather | solution.py:114
  415.9 11.7 fusion.130
  427.6 33.5 %all-gather.29.cloned.1.call-done = bf16[2048,1408]{1,0:T(8,128)(2,1)} async-done(((bf16[256,1408]{1,0:T(8,128)(2,1)}), bf16[2048,1408]{1,0:T(8,128)(2,1)}) %all-gather.29.cloned.1.call-update) | async-done | bytes 5767184 | tf_op jit(solution)/shard_map/all_gather | solution.py:115
  461.0 11.7 fusion.131
  472.7 34.3 %all-gather.31.cloned.1.call-done = bf16[1408,2048]{1,0:T(8,128)(2,1)} async-done(((bf16[1408,256]{1,0:T(8,128)(2,1)}), bf16[1408,2048]{1,0:T(8,128)(2,1)}) %all-gather.31.cloned.1.call-update) | async-done | bytes 5767184 | tf_op jit(solution)/shard_map/all_gather | solution.py:116
  507.1 15.6 multiply_convert_fusion.1
  522.7 10.9 fusion.132
  533.6 8.7 add_convert_fusion
  542.4 286.8 %all-gather.33.cloned.1.call-done = bf16[4096,2048]{1,0:T(8,128)(2,1)} async-done(((bf16[1024,2048]{1,0:T(8,128)(2,1)}), bf16[4096,2048]{1,0:T(8,128)(2,1)}) %all-gather.33.cloned.1.call-update) | async-done | bytes 16777232 | tf_op jit(solution)/shard_map/all_gather | solution.py:10
  829.2 12.1 reduce_sum.130
  841.3 8.2 fusion.62
  849.6 9.6 fusion.86
  859.3 144.5 %while.32 = (s32[]{:T(128)}, f32[1,2048,512]{1,2,0:T(8,128)}, f32[2,512,4,256]{3,1,0,2:T(8,128)}, s32[2]{0:T(128)S(1)}, s32[1024]{0:T(1024)S(1)}, /*index=5*/s32...) while((s32[]{:T(128)}, f32[1,2048,512]{1,2,0:T(8,128)}, ...), condition=%wide.region_15.16_spmd.clone, body=%wide.region_12.15_spmd.clone.sunk | while | flops 10809767936 | bytes 248594592 | solution.py:250
  862.0 9.4 fusion.190
  874.2 13.2 fusion.193
  887.5 15.9 fusion.194
  903.3 8.0 fusion.195
  933.3 9.4 fusion.190
  945.6 13.2 fusion.193
  958.8 15.9 fusion.194
  974.7 8.0 fusion.195
  1007.9 11.0 convolution_convert_fusion.3
  1032.1 11.2 convolution_convert_fusion.2
  1045.1 10.8 convolution_convert_fusion.1
  1057.7 10.8 convolution_convert_fusion
  1076.1 14.8 convolution_convert_fusion.4
  1091.0 194.5 %all-reduce.10.cloned.1.call-done = (bf16[1024,2048]{1,0:T(8,128)(2,1)}, bf16[1024,1024]{0,1:T(8,128)(2,1)}, bf16[1,1024,512]{1,2,0:T(8,128)(2,1)}) async-done(((bf16[1024,2048]{1,0:T(8,128)(2,1)}, bf16[1024,1024]{0,1:T(8,128)(2,1)}, bf16[1,1024,512]{1,2,0:T(8,128)(2,1)}), (bf16[1024,2048]{1,0:T(8,128)(2,1)}, bf16[1024,1024]{0,1:T(8,128)(2,1)}, ...) | async-done | bytes 7340048 | tf_op jit(solution)/shard_map/psum | solution.py:198
  1315.6 31.1 %reduce-scatter.22.cloned.1.call-done = bf16[256,1408]{1,0:T(8,128)(2,1)} async-done(((bf16[2048,1408]{1,0:T(8,128)(2,1)}), bf16[256,1408]{1,0:T(8,128)(2,1)}) %reduce-scatter.22.cloned.1.call-update) | async-done | bytes 720912 | tf_op jit(solution)/shard_map/reduce_scatter | solution.py:313
  1349.0 60.0 %reduce-scatter.24.cloned.1.call-done = bf16[256,1408]{1,0:T(8,128)(2,1)} async-done(((bf16[2048,1408]{1,0:T(8,128)(2,1)}), bf16[256,1408]{1,0:T(8,128)(2,1)}) %reduce-scatter.24.cloned.1.call-update) | async-done | bytes 720912 | tf_op jit(solution)/shard_map/reduce_scatter | solution.py:316
  1411.3 59.9 %reduce-scatter.26.cloned.1.call-done = bf16[1408,256]{1,0:T(8,128)(2,1)} async-done(((bf16[1408,2048]{1,0:T(8,128)(2,1)}), bf16[1408,256]{1,0:T(8,128)(2,1)}) %reduce-scatter.26.cloned.1.call-update) | async-done | bytes 720912 | tf_op jit(solution)/shard_map/reduce_scatter | solution.py:319
  1473.5 42.0 %reduce-scatter.14.cloned.1.call-done = bf16[128,1024]{1,0:T(8,128)(2,1)} async-done(((bf16[1024,1024]{1,0:T(8,128)(2,1)}), bf16[128,1024]{1,0:T(8,128)(2,1)}) %reduce-scatter.14.cloned.1.call-update) | async-done | bytes 262160 | tf_op jit(solution)/shard_map/reduce_scatter | solution.py:298
  1517.3 53.1 %reduce-scatter.20.cloned.1.call-done = bf16[1024,256]{1,0:T(8,128)(2,1)} async-done(((bf16[1024,2048]{1,0:T(8,128)(2,1)}), bf16[1024,256]{1,0:T(8,128)(2,1)}) %reduce-scatter.20.cloned.1.call-update) | async-done | bytes 524304 | tf_op jit(solution)/shard_map/reduce_scatter | solution.py:307
  1579.9 8.6 fusion.66
  1588.6 23.3 %all-reduce.3 = (bf16[2048]{0:T(1024)(128)(2,1)S(1)}, bf16[1024]{0:T(1024)(128)(2,1)S(1)}, bf16[2048]{0:T(1024)(128)(2,1)S(1)}) all-reduce(bf16[2048]{0:T(1024)(128)(2,1)S(1)} %get-tuple-element.449, bf16[1024]{0:T(1024)(128)(2,1)} %get-tuple-element.451, ...), channel_id=4, replica_groups=mesh['fsdp'=4,'ctx'=2,'tp'=4] {'fsdp','ctx'}, use_global_device_ids=true, to_apply=%region_22.23.clone | all-reduce | flops 5120 | bytes 20480
  1613.7 17.0 fusion.79
  1632.3 17.0 reduce-scatter.18.cloned.1.call-done
  1650.9 52.9 %reduce-scatter.12.cloned.1.call-done = bf16[256,1024]{1,0:T(8,128)(2,1)} async-done(((bf16[2048,1024]{1,0:T(8,128)(2,1)}), bf16[256,1024]{1,0:T(8,128)(2,1)}) %reduce-scatter.12.cloned.1.call-update) | async-done | bytes 524304 | tf_op jit(solution)/shard_map/reduce_scatter | solution.py:292
  (280 shorter events, 217.6 us)
Async XLA Ops:
  7.2 28.8 %all-gather.19.cloned.1.call-start = ((), (), s32[]{:S(2)}) async-start(), calls=%async_computation.11 | async-start | bytes 1179648 | tf_op jit(solution)/shard_map/all_gather | solution.py:110
  7.9 53.4 %all-gather.21.cloned.1.call-start = ((), (), s32[]{:S(2)}) async-start(), calls=%async_computation.12 | async-start | bytes 1179648 | tf_op jit(solution)/shard_map/all_gather | solution.py:111
  8.7 70.7 %all-gather.23.cloned.1.call-start = ((), (), s32[]{:S(2)}) async-start(), calls=%async_computation.13 | async-start | bytes 3145728 | tf_op jit(solution)/shard_map/all_gather | solution.py:147
  19.8 96.9 %copy-start.24 = (f32[8,1,256]{2,1,0:T(1,128)}, f32[8,1,256]{2,1,0:T(1,128)S(1)}, u32[]{:S(2)}) copy-start(f32[8,1,256]{2,1,0:T(1,128)S(1)} %convert_element_type.304) | copy-start | bytes 24580
  19.8 48.4 %copy-start.39 = (f32[128]{0:T(128)}, f32[128]{0:T(128)S(1)}, u32[]{:S(2)}) copy-start(f32[128]{0:T(128)S(1)} %multiply_exponential_fusion) | copy-start | bytes 1540
  19.8 48.3 %copy-start.26 = (f32[1024]{0:T(1024)}, f32[1024]{0:T(1024)S(1)}, u32[]{:S(2)}) copy-start(f32[1024]{0:T(1024)S(1)} %fusion.118) | copy-start | bytes 12292
  23.0 93.7 %copy-start.34 = (f32[1024]{0:T(1024)}, f32[1024]{0:T(1024)S(1)}, u32[]{:S(2)}) copy-start(f32[1024]{0:T(1024)S(1)} %add_rsqrt_fusion.2) | copy-start | bytes 12292
  65.3 13.8 copy-start.42
  66.4 50.3 %all-gather.15.cloned.1.call-start = ((), (), s32[]{:S(2)}) async-start(), calls=%async_computation.9 | async-start | bytes 4718592 | tf_op jit(solution)/shard_map/all_gather | solution.py:107
  67.0 79.2 %all-gather.17.cloned.1.call-start = ((), (), s32[]{:S(2)}) async-start(), calls=%async_computation.10 | async-start | bytes 2359296 | tf_op jit(solution)/shard_map/all_gather | solution.py:109
  67.5 139.9 %all-gather.25.cloned.1.call-start = ((), (), s32[]{:S(2)}) async-start(), calls=%async_computation.14 | async-start | bytes 4718592 | tf_op jit(solution)/shard_map/all_gather | solution.py:112
  68.1 303.7 %all-reduce.8.cloned.1.call-start = ((), (), s32[]{:S(2)}) async-start(), calls=%async_computation.15 | async-start | bytes 8388608 | tf_op jit(solution)/shard_map/psum | solution.py:188
  70.1 89.7 %copy-start.14 = (f32[1024,128]{1,0:T(8,128)}, f32[1024,128]{1,0:T(8,128)S(1)}, u32[]{:S(2)}) copy-start(f32[1024,128]{1,0:T(8,128)S(1)} %get-tuple-element.518) | copy-start | bytes 1572868
  70.1 89.7 %copy-start.16 = (f32[1024,128]{1,0:T(8,128)}, f32[1024,128]{1,0:T(8,128)S(1)}, u32[]{:S(2)}) copy-start(f32[1024,128]{1,0:T(8,128)S(1)} %get-tuple-element.519) | copy-start | bytes 1572868
  79.1 67.1 %copy-start.30 = (f32[8,1,128]{2,1,0:T(1,128)}, f32[8,1,128]{2,1,0:T(1,128)S(1)}, u32[]{:S(2)}) copy-start(f32[8,1,128]{2,1,0:T(1,128)S(1)} %convert_element_type.305) | copy-start | bytes 12292
  126.8 24.7 %copy-start.32 = (f32[1024]{0:T(1024)}, f32[1024]{0:T(1024)S(1)}, u32[]{:S(2)}) copy-start(f32[1024]{0:T(1024)S(1)} %add_rsqrt_fusion.1) | copy-start | bytes 12292
  216.8 199.1 %all-gather.27.cloned.1.call-start = ((), (), s32[]{:S(2)}) async-start(), calls=%async_computation.16 | async-start | bytes 6488064 | tf_op jit(solution)/shard_map/all_gather | solution.py:114
  217.6 243.5 %all-gather.29.cloned.1.call-start = ((), (), s32[]{:S(2)}) async-start(), calls=%async_computation.17 | async-start | bytes 6488064 | tf_op jit(solution)/shard_map/all_gather | solution.py:115
  218.3 288.8 %all-gather.31.cloned.1.call-start = ((), (), s32[]{:S(2)}) async-start(), calls=%async_computation.18 | async-start | bytes 6488064 | tf_op jit(solution)/shard_map/all_gather | solution.py:116
  218.9 610.3 %all-gather.33.cloned.1.call-start = ((), (), s32[]{:S(2)}) async-start(), calls=%async_computation.28 | async-start | bytes 20971520 | tf_op jit(solution)/shard_map/all_gather | solution.py:10
  227.8 621.8 %copy-start.22 = (f32[8,1,256]{2,1,0:T(1,128)}, f32[8,1,256]{2,1,0:T(1,128)S(1)}, u32[]{:S(2)}) copy-start(f32[8,1,256]{2,1,0:T(1,128)S(1)} %convert_element_type.306) | copy-start | bytes 24580
  376.9 472.7 %copy-start.28 = (f32[1024]{0:T(1024)}, f32[1024]{0:T(1024)S(1)}, u32[]{:S(2)}) copy-start(f32[1024]{0:T(1024)S(1)} %add_rsqrt_fusion) | copy-start | bytes 12292
  522.7 10.9 copy-start.43
  542.3 488.0 %reduce-scatter.10.cloned.1.call-start = ((), (), s32[]{:S(2)}) async-start(), calls=%async_computation.19 | async-start | bytes 3145728 | tf_op jit(solution)/shard_map/reduce_scatter | solution.py:263
  887.4 15.9 copy-start.10
  887.4 24.0 %slice-start = ((s8[16777216]{0:T(1024)(128)(4,1)}), s8[4194304]{0:T(1024)(128)(4,1)S(1)}, s32[]{:S(2)}) async-start(s8[16777216]{0:T(1024)(128)(4,1)} %bitcast.331), calls=%async_computation.30 | async-start | bytes 8388608 | tf_op jit(solution)/shard_map/while
  887.4 24.0 %slice-start.1 = ((s8[16777216]{0:T(1024)(128)(4,1)}), s8[4194304]{0:T(1024)(128)(4,1)S(1)}, s32[]{:S(2)}) async-start(s8[16777216]{0:T(1024)(128)(4,1)} %bitcast.331), calls=%async_computation.31 | async-start | bytes 8388608 | tf_op jit(solution)/shard_map/while
  887.4 24.0 %slice-start.2 = ((s8[16777216]{0:T(1024)(128)(4,1)}), s8[4194304]{0:T(1024)(128)(4,1)S(1)}, s32[]{:S(2)}) async-start(s8[16777216]{0:T(1024)(128)(4,1)} %bitcast.331), calls=%async_computation.32 | async-start | bytes 8388608 | tf_op jit(solution)/shard_map/while
  958.8 15.9 copy-start.10
  958.8 24.0 %slice-start = ((s8[16777216]{0:T(1024)(128)(4,1)}), s8[4194304]{0:T(1024)(128)(4,1)S(1)}, s32[]{:S(2)}) async-start(s8[16777216]{0:T(1024)(128)(4,1)} %bitcast.331), calls=%async_computation.30 | async-start | bytes 8388608 | tf_op jit(solution)/shard_map/while
  958.8 24.0 %slice-start.1 = ((s8[16777216]{0:T(1024)(128)(4,1)}), s8[4194304]{0:T(1024)(128)(4,1)S(1)}, s32[]{:S(2)}) async-start(s8[16777216]{0:T(1024)(128)(4,1)} %bitcast.331), calls=%async_computation.31 | async-start | bytes 8388608 | tf_op jit(solution)/shard_map/while
  958.8 24.0 %slice-start.2 = ((s8[16777216]{0:T(1024)(128)(4,1)}), s8[4194304]{0:T(1024)(128)(4,1)S(1)}, s32[]{:S(2)}) async-start(s8[16777216]{0:T(1024)(128)(4,1)} %bitcast.331), calls=%async_computation.32 | async-start | bytes 8388608 | tf_op jit(solution)/shard_map/while
  1007.8 277.7 %all-reduce.10.cloned.1.call-start = ((), (), s32[]{:S(2)}) async-start(), calls=%async_computation.29 | async-start | bytes 14680064 | tf_op jit(solution)/shard_map/psum | solution.py:198
  1007.8 11.0 copy-start.15
  1007.8 11.0 copy-start.17
  1030.3 316.4 %reduce-scatter.22.cloned.1.call-start = ((), (), s32[]{:S(2)}) async-start(), calls=%async_computation.25 | async-start | bytes 6488064 | tf_op jit(solution)/shard_map/reduce_scatter | solution.py:313
  1043.3 365.7 %reduce-scatter.24.cloned.1.call-start = ((), (), s32[]{:S(2)}) async-start(), calls=%async_computation.26 | async-start | bytes 6488064 | tf_op jit(solution)/shard_map/reduce_scatter | solution.py:316
  1055.9 415.3 %reduce-scatter.26.cloned.1.call-start = ((), (), s32[]{:S(2)}) async-start(), calls=%async_computation.27 | async-start | bytes 6488064 | tf_op jit(solution)/shard_map/reduce_scatter | solution.py:319
  1068.6 446.9 %reduce-scatter.14.cloned.1.call-start = ((), (), s32[]{:S(2)}) async-start(), calls=%async_computation.21 | async-start | bytes 2359296 | tf_op jit(solution)/shard_map/reduce_scatter | solution.py:298
  1075.9 494.6 %reduce-scatter.20.cloned.1.call-start = ((), (), s32[]{:S(2)}) async-start(), calls=%async_computation.24 | async-start | bytes 4718592 | tf_op jit(solution)/shard_map/reduce_scatter | solution.py:307
  1090.9 196.2 %copy-start.27 = (f32[1024]{0:T(1024)S(1)}, f32[1024]{0:T(1024)}, u32[]{:S(2)}) copy-start(f32[1024]{0:T(1024)} %copy-done.26) | copy-start | bytes 12292
  1090.9 196.2 %copy-start.40 = (f32[128]{0:T(128)S(1)}, f32[128]{0:T(128)}, u32[]{:S(2)}) copy-start(f32[128]{0:T(128)} %copy-done.39) | copy-start | bytes 1540
  1090.9 198.5 %copy-start.25 = (f32[8,1,256]{2,1,0:T(1,128)S(1)}, f32[8,1,256]{2,1,0:T(1,128)}, u32[]{:S(2)}) copy-start(f32[8,1,256]{2,1,0:T(1,128)} %copy-done.24) | copy-start | bytes 24580
  1090.9 198.5 %copy-start.35 = (f32[1024]{0:T(1024)S(1)}, f32[1024]{0:T(1024)}, u32[]{:S(2)}) copy-start(f32[1024]{0:T(1024)} %copy-done.34) | copy-start | bytes 12292
  1091.0 539.7 %reduce-scatter.16.cloned.1.call-start = ((), (), s32[]{:S(2)}) async-start(), calls=%async_computation.22 | async-start | bytes 1179648 | tf_op jit(solution)/shard_map/reduce_scatter | solution.py:301
  1292.3 357.0 %reduce-scatter.18.cloned.1.call-start = ((), (), s32[]{:S(2)}) async-start(), calls=%async_computation.23 | async-start | bytes 1179648 | tf_op jit(solution)/shard_map/reduce_scatter | solution.py:304
  1300.2 403.6 %reduce-scatter.12.cloned.1.call-start = ((), (), s32[]{:S(2)}) async-start(), calls=%async_computation.20 | async-start | bytes 4718592 | tf_op jit(solution)/shard_map/reduce_scatter | solution.py:292
  1315.6 256.9 %copy-start.21 = (bf16[2048,256]{1,0:T(8,128)(2,1)S(1)}, bf16[2048,256]{1,0:T(8,128)(2,1)}, u32[]{:S(2)}) copy-start(bf16[2048,256]{1,0:T(8,128)(2,1)} %all-gather.19.cloned.1.call-done) | copy-start | bytes 3145732
  (36 other events, 189.3 us)
Sparse Core Ops, SparseCore 0:
  9.9 26.0 all-gather.18
  37.9 23.3 all-gather.20
  66.5 10.5 all-gather.22
  78.8 37.7 all-gather.14
  118.4 27.7 all-gather.16
  147.9 37.3 all-gather.24
  216.9 154.8 all-reduce.7
  373.7 42.1 all-gather.26
  417.8 43.1 all-gather.28
  462.8 44.2 all-gather.30
  542.4 286.7 all-gather.32
  1007.9 7.7 reduce-scatter.9
  1030.4 254.9 all-reduce.9
  1288.8 57.8 reduce-scatter.21
  1350.0 59.0 reduce-scatter.23
  1412.3 58.8 reduce-scatter.25
  1474.4 41.1 reduce-scatter.13
  1519.3 51.0 reduce-scatter.19
  1574.2 36.1 reduce-scatter.15
  1613.4 35.8 reduce-scatter.17
  1652.6 51.1 reduce-scatter.11
